TPU v7x, 32 devices: a whole 2x2x4 slice. The times are simulated.
32 devices in a mesh: dp: 4 (over y, core), row: 4 (over z), col: 2 (over x).
Axes of the slice: x: 2, y: 2, z: 4, core: 2. Of those that a mesh axis runs over, the one named last changes fastest.
Arguments:
- inputs: bfloat16 [4096, 1024], P(('dp', 'col'), 'row'), may hold values from -6 to 6
- cotangent: bfloat16 [4096, 1024], P(('dp', 'col'), 'row'), may hold values from -6 to 6
- seg_parent: int32 [52], P('dp'), may hold values from 0 to 51, as said below
- token_depth: int32 [4096], P('dp'), may hold values from 0 to 383, as said below
- ln1_gain: float32 [1024], P('row'), may hold values from 0.25 to 1.75
- ln1_bias: float32 [1024], P('row'), may hold values from -1.5 to 1.5
- w_qkv: bfloat16 [1024, 3, 1024], P('row', None, 'col'), may hold values from -0.1875 to 0.1875
- b_qv: float32 [2, 1024], P(None, 'col'), may hold values from -1.5 to 1.5
- w_out: bfloat16 [1024, 1024], P('col', 'row'), may hold values from -0.5 to 0.5
- b_out: float32 [1024], P('row'), may hold values from -1.5 to 1.5
- ln2_gain: float32 [1024], P('row'), may hold values from 0.25 to 1.75
- ln2_bias: float32 [1024], P('row'), may hold values from -1.5 to 1.5
- w_up: bfloat16 [1024, 4096], P('row', 'col'), may hold values from -0.1875 to 0.1875
- b_up: float32 [4096], P('col'), may hold values from -1.5 to 1.5
- w_down: bfloat16 [4096, 1024], P('col', 'row'), may hold values from -0.125 to 0.125
- b_down: float32 [1024], P('row'), may hold values from -1.5 to 1.5
Outputs:
- result: float32 [4096, 1024], P(('dp', 'col'), 'row')
- input_grad: float32 [4096, 1024], P(('dp', 'col'), 'row')
- grad_ln1_gain: float32 [1024], P('row')
- grad_ln1_bias: float32 [1024], P('row')
- grad_w_qkv: float32 [1024, 3, 1024], P('row', None, 'col')
- grad_b_qv: float32 [2, 1024], P(None, 'col')
- grad_w_out: float32 [1024, 1024], P('col', 'row')
- grad_b_out: float32 [1024], P('row')
- grad_ln2_gain: float32 [1024], P('row')
- grad_ln2_bias: float32 [1024], P('row')
- grad_w_up: float32 [1024, 4096], P('row', 'col')
- grad_b_up: float32 [4096], P('col')
- grad_w_down: float32 [4096, 1024], P('col', 'row')
- grad_b_down: float32 [1024], P('row')
Inputs may be any that keep to these rules, and one draw needn't show every extreme that they name: `seg_parent`: tree t holds tokens t * 1024 to (t + 1) * 1024 - 1 and segments 13 t to 13 t + 12, laid out as segment(i) says: segment 13 t is the trunk of 256 tokens and is its own parent; four of the other twelve are branches with the trunk as parent, eight are leaves, two for every branch, with that branch as parent; segment 13 t + 12 is a branch; which ids play the other parts is drawn. `token_depth`: the token at offset j of its segment has depth j in a trunk, 256 + j in a branch and 320 + j in a leaf.
All inputs are finite; a program needn't handle non-finite values.
Results may differ from a plain program's by a relative error of at most 0.011.
Values may be sent and summed in bfloat16 or wider, within the bound.
A program may use at most 192 MiB of HBM per device.

v0:
```python
import math
import jax
import jax.numpy as jnp
from jax import lax
from jax.sharding import PartitionSpec as P

HD = 128
EPS = 1e-05
MASKED = -1e30


def gelu_value(values):
    return 0.5 * values * (1.0 + jax.scipy.special.erf(values / math.sqrt(2.0)))


def gelu_slope(values):
    return 0.5 * (1.0 + jax.scipy.special.erf(values / math.sqrt(2.0))) + values * jnp.exp(
        -0.5 * values * values
    ) / math.sqrt(2.0 * math.pi)


def width_sums(first_term, second_term):
    return lax.psum((jnp.sum(first_term, axis=1), jnp.sum(second_term, axis=1)), "row")


def normalize(values, norm_gain, norm_bias, feature_count):
    row_total, square = width_sums(values, values * values)
    row_mean = row_total / feature_count
    inv_std = lax.rsqrt(square / feature_count - row_mean * row_mean + EPS)
    normed = (values - row_mean[:, None]) * inv_std[:, None]
    return (normed, inv_std, (normed * norm_gain + norm_bias).astype(jnp.bfloat16))


def normalize_back(upstream, normed, inv_std, norm_gain, feature_count):
    spread = upstream * norm_gain
    row_total, cross_sum = width_sums(spread, spread * normed)
    return inv_std[:, None] * (
        spread - row_total[:, None] / feature_count - normed * (cross_sum[:, None] / feature_count)
    )


def contract(left_op, right_op, flipped):
    if flipped:
        return lax.dot_general(
            left_op, right_op, (((1,), (1,)), ((), ())), preferred_element_type=jnp.float32
        )
    return jnp.dot(left_op, right_op, preferred_element_type=jnp.float32)


def outer_sum(left_op, right_op):
    return lax.dot_general(
        left_op, right_op, (((0,), (0,)), ((), ())), preferred_element_type=jnp.float32
    )


def across_rows(operand, weight_block, flipped):
    gathered = lax.all_gather(operand, "col", axis=0, tiled=True)
    row_count = gathered.shape[0] // lax.axis_size("row")

    def partial_term(row_start, row_num):
        return contract(gathered, weight_block, flipped)

    return (
        lax.psum_scatter(
            partial_term(jnp.int32(0), row_count * lax.axis_size("row")),
            "row",
            scatter_dimension=0,
            tiled=True,
        ),
        gathered,
    )


def across_cols(operand, weight_block, flipped):
    gathered = lax.all_gather(operand, "row", axis=0, tiled=True)
    row_count = gathered.shape[0] // lax.axis_size("col")

    def partial_term(row_start, row_num):
        return contract(gathered, weight_block, flipped)

    return (
        lax.psum_scatter(
            partial_term(jnp.int32(0), row_count * lax.axis_size("col")),
            "col",
            scatter_dimension=0,
            tiled=True,
        ),
        gathered,
    )


def tree_labels(seg_parent, token_depth):
    seg_count = seg_parent.shape[0]
    tree_len = token_depth.shape[0]
    seg_len = tree_len // 16
    slot_ids = jnp.arange(seg_count, dtype=jnp.int32)
    where_at = jnp.arange(tree_len, dtype=jnp.int32)
    segment = jnp.where(where_at < 4 * seg_len, 0, 1 + (where_at - 4 * seg_len) // seg_len)
    parent_local = seg_parent - lax.axis_index("dp") * seg_count
    parent_one = jnp.sum(
        jnp.where(segment[:, None] == slot_ids[None, :], parent_local[None, :], 0), axis=1
    )
    parent_two = jnp.sum(
        jnp.where(parent_one[:, None] == slot_ids[None, :], parent_local[None, :], 0), axis=1
    )
    return (segment, parent_one, parent_two, token_depth)


def block_scores(query_block, key_rows, labels, query_start, slopes):
    segment, parent_one, parent_two, token_depth = labels
    block_size = query_block.shape[0]
    query_seg = lax.dynamic_slice_in_dim(segment, query_start, block_size, 0)
    query_one = lax.dynamic_slice_in_dim(parent_one, query_start, block_size, 0)
    query_two = lax.dynamic_slice_in_dim(parent_two, query_start, block_size, 0)
    query_depth = lax.dynamic_slice_in_dim(token_depth, query_start, block_size, 0)
    allowed = (
        (segment[None, :] == query_seg[:, None])
        | (segment[None, :] == query_one[:, None])
        | (segment[None, :] == query_two[:, None])
    ) & (token_depth[None, :] <= query_depth[:, None])
    score_scale = query_block.shape[2] ** (-0.5)
    raw = jnp.einsum("qhd,khd->hqk", query_block, key_rows, preferred_element_type=jnp.float32)
    distance = (query_depth[:, None] - token_depth[None, :]).astype(jnp.float32)
    scores = raw * score_scale - slopes[:, None, None] * distance[None]
    return jnp.where(allowed[None], scores, MASKED)


def attention_forward(queries, key_rows, value_rows, labels, slopes, offset):
    block_size = min(512, queries.shape[0])
    blocks = queries.shape[0] // block_size

    def one_block(block_index):
        block_first = block_index * block_size
        query_block = lax.dynamic_slice_in_dim(queries, block_first, block_size, 0)
        scores = block_scores(query_block, key_rows, labels, offset + block_first, slopes)
        top_score = jnp.max(scores, axis=2, keepdims=True)
        weights = jnp.exp(scores - top_score)
        weight_total = jnp.sum(weights, axis=2, keepdims=True)
        probs = (weights / weight_total).astype(jnp.bfloat16)
        mixed = jnp.einsum("hqk,khd->qhd", probs, value_rows, preferred_element_type=jnp.float32)
        return (mixed, (top_score + jnp.log(weight_total))[:, :, 0])

    return lax.map(one_block, jnp.arange(blocks, dtype=jnp.int32))


def attention_backward(
    queries, key_rows, value_rows, grad_mixed, log_total, labels, slopes, offset
):
    block_size = min(512, queries.shape[0])
    blocks = queries.shape[0] // block_size
    score_scale = queries.shape[2] ** (-0.5)

    def one_block(carry, items):
        key_grad, value_grad = carry
        block_index, block_total = items
        block_first = block_index * block_size
        query_block = lax.dynamic_slice_in_dim(queries, block_first, block_size, 0)
        grad_block = lax.dynamic_slice_in_dim(grad_mixed, block_first, block_size, 0)
        scores = block_scores(query_block, key_rows, labels, offset + block_first, slopes)
        probs = jnp.exp(scores - block_total[:, :, None])
        grad_probs = jnp.einsum(
            "qhd,khd->hqk", grad_block, value_rows, preferred_element_type=jnp.float32
        )
        centre = jnp.sum(probs * grad_probs, axis=2, keepdims=True)
        grad_scores = (probs * (grad_probs - centre)).astype(jnp.bfloat16)
        query_grad = (
            jnp.einsum("hqk,khd->qhd", grad_scores, key_rows, preferred_element_type=jnp.float32)
            * score_scale
        )
        key_grad = (
            key_grad
            + jnp.einsum(
                "hqk,qhd->khd", grad_scores, query_block, preferred_element_type=jnp.float32
            )
            * score_scale
        )
        value_grad = value_grad + jnp.einsum(
            "hqk,qhd->khd",
            probs.astype(jnp.bfloat16),
            grad_block,
            preferred_element_type=jnp.float32,
        )
        return ((key_grad, value_grad), query_grad)

    empty = jnp.zeros(key_rows.shape, jnp.float32)
    (key_grad, value_grad), query_grad = lax.scan(
        one_block, (empty, empty), (jnp.arange(blocks, dtype=jnp.int32), log_total)
    )
    return (key_grad, value_grad, query_grad)


def on_device(
    inputs,
    cotangent,
    seg_parent,
    token_depth,
    ln1_gain,
    ln1_bias,
    w_qkv,
    b_qv,
    w_out,
    b_out,
    ln2_gain,
    ln2_bias,
    w_up,
    b_up,
    w_down,
    b_down,
):
    feature_count = inputs.shape[1] * lax.axis_size("row")
    col_width = w_qkv.shape[2]
    heads_here = col_width // HD
    qkv_flat = w_qkv.reshape(w_qkv.shape[0], 3 * col_width)
    labels = tree_labels(seg_parent, token_depth)
    heads_seen = lax.axis_index("col") * heads_here + jnp.arange(heads_here, dtype=jnp.int32)
    slopes = jnp.exp2(-(heads_seen + 1).astype(jnp.float32))
    states = inputs.astype(jnp.float32)
    normed_one, inv_one, entry_one = normalize(states, ln1_gain, ln1_bias, feature_count)
    projected, entry_one_all = across_rows(entry_one, qkv_flat, False)
    tok_rows = projected.shape[0]
    projected = projected.reshape(tok_rows, 3, col_width)
    queries = (projected[:, 0] + b_qv[0]).astype(jnp.bfloat16)
    keys_here = projected[:, 1].astype(jnp.bfloat16)
    values_here = (projected[:, 2] + b_qv[1]).astype(jnp.bfloat16)
    pair_all = lax.all_gather(
        jnp.stack([keys_here, values_here], axis=1), "row", axis=0, tiled=True
    )
    key_rows = pair_all[:, 0].reshape(-1, heads_here, HD)
    value_rows = pair_all[:, 1].reshape(-1, heads_here, HD)
    query_heads = queries.reshape(tok_rows, heads_here, HD)
    offset = lax.axis_index("row") * tok_rows
    mixed, log_total = attention_forward(query_heads, key_rows, value_rows, labels, slopes, offset)
    mixed = mixed.reshape(tok_rows, col_width).astype(jnp.bfloat16)
    attn_out, mixed_all = across_cols(mixed, w_out, False)
    middle = states + attn_out + b_out
    normed_two, inv_two, entry_two = normalize(middle, ln2_gain, ln2_bias, feature_count)
    hidden_pre, entry_two_all = across_rows(entry_two, w_up, False)
    hidden_pre = hidden_pre + b_up
    hidden = gelu_value(hidden_pre).astype(jnp.bfloat16)
    ffn_out, hidden_all = across_cols(hidden, w_down, False)
    result = middle + ffn_out + b_down
    grad_hidden, down_all = across_rows(cotangent, w_down, True)
    grad_pre = (grad_hidden * gelu_slope(hidden_pre)).astype(jnp.bfloat16)
    grad_entry_two, pre_all = across_cols(grad_pre, w_up, True)
    grad_middle = cotangent.astype(jnp.float32) + normalize_back(
        grad_entry_two, normed_two, inv_two, ln2_gain, feature_count
    )
    grad_branch = grad_middle.astype(jnp.bfloat16)
    grad_mixed, branch_all = across_rows(grad_branch, w_out, True)
    grad_mixed = grad_mixed.astype(jnp.bfloat16).reshape(tok_rows, heads_here, HD)
    key_grad, value_grad, query_grad = attention_backward(
        query_heads, key_rows, value_rows, grad_mixed, log_total, labels, slopes, offset
    )
    kv_grads = lax.psum_scatter(
        jnp.stack([key_grad.reshape(-1, col_width), value_grad.reshape(-1, col_width)], axis=1),
        "row",
        scatter_dimension=0,
        tiled=True,
    )
    grad_projected = jnp.stack(
        [
            query_grad.reshape(tok_rows, col_width).astype(jnp.bfloat16),
            kv_grads[:, 0].astype(jnp.bfloat16),
            kv_grads[:, 1].astype(jnp.bfloat16),
        ],
        axis=1,
    )
    grad_entry_one, proj_all = across_cols(
        grad_projected.reshape(tok_rows, 3 * col_width), qkv_flat, True
    )
    input_grad = grad_middle + normalize_back(
        grad_entry_one, normed_one, inv_one, ln1_gain, feature_count
    )
    proj_sums = jnp.sum(proj_all.astype(jnp.float32), axis=0).reshape(3, col_width)
    weight_terms = (
        outer_sum(entry_one_all, proj_all).reshape(w_qkv.shape),
        jnp.stack([proj_sums[0], proj_sums[2]], axis=0),
        outer_sum(mixed_all, branch_all),
        jnp.sum(branch_all.astype(jnp.float32), axis=0),
        outer_sum(entry_two_all, pre_all),
        jnp.sum(pre_all.astype(jnp.float32), axis=0),
        outer_sum(hidden_all, down_all),
        jnp.sum(down_all.astype(jnp.float32), axis=0),
    )
    (
        grad_w_qkv,
        grad_b_qv,
        grad_w_out,
        grad_b_out,
        grad_w_up,
        grad_b_up,
        grad_w_down,
        grad_b_down,
    ) = lax.psum(
        (
            weight_terms[0],
            weight_terms[1],
            weight_terms[2],
            weight_terms[3],
            weight_terms[4],
            weight_terms[5],
            weight_terms[6],
            weight_terms[7],
        ),
        "dp",
    )
    norm_terms = (
        jnp.sum(grad_entry_one * normed_one, axis=0),
        jnp.sum(grad_entry_one, axis=0),
        jnp.sum(grad_entry_two * normed_two, axis=0),
        jnp.sum(grad_entry_two, axis=0),
    )
    grad_ln1_gain, grad_ln1_bias, grad_ln2_gain, grad_ln2_bias = lax.psum(
        (norm_terms[0], norm_terms[1], norm_terms[2], norm_terms[3]), ("dp", "col")
    )
    return (
        result,
        input_grad,
        grad_ln1_gain,
        grad_ln1_bias,
        grad_w_qkv,
        grad_b_qv,
        grad_w_out,
        grad_b_out,
        grad_ln2_gain,
        grad_ln2_bias,
        grad_w_up,
        grad_b_up,
        grad_w_down,
        grad_b_down,
    )


def solution(mesh):
    placed = (
        P(("dp", "col"), "row"),
        P(("dp", "col"), "row"),
        P("dp"),
        P("dp"),
        P("row"),
        P("row"),
        P("row", None, "col"),
        P(None, "col"),
        P("col", "row"),
        P("row"),
        P("row"),
        P("row"),
        P("row", "col"),
        P("col"),
        P("col", "row"),
        P("row"),
    )
    return jax.shard_map(
        on_device,
        mesh=mesh,
        in_specs=placed,
        out_specs=(
            P(("dp", "col"), "row"),
            P(("dp", "col"), "row"),
            P("row"),
            P("row"),
            P("row", None, "col"),
            P(None, "col"),
            P("col", "row"),
            P("row"),
            P("row"),
            P("row"),
            P("row", "col"),
            P("col"),
            P("col", "row"),
            P("row"),
        ),
        check_vma=False,
    )
```

profile of v0, /device:TPU:0, one launch (start us, length us, event | category | flops | bytes accessed | tf_op | source)
XLA Modules:
  0.0 1127.7 jit_solution(2528115706905828047)
XLA Ops:
  8.5 13.5 %all-reduce.4 = (f32[512]{0:T(512)S(1)}, f32[512]{0:T(512)S(1)}) all-reduce(f32[512]{0:T(512)S(1)} %get-tuple-element.134, f32[512]{0:T(512)S(1)} %get-tuple-element.133), channel_id=1, replica_groups=mesh['dp'=4,'row'=4,'col'=2] {'row'}, use_global_device_ids=true, to_apply=%region_3.4 | all-reduce | flops 1024 | bytes 8192 | tf_op jit(solution)/shard_map/psum | solution.py:23
  23.1 7.0 all_gather.27
  31.8 3.7 fusion.46
  36.2 108.4 %reduce-scatter.10.cloned.1.call-done = f32[256,1536]{1,0:T(8,128)} async-done(((f32[1024,1536]{1,0:T(8,128)}), f32[256,1536]{1,0:T(8,128)}) %reduce-scatter.10.cloned.1.call-update) | async-done | bytes 1572880 | tf_op jit(solution)/shard_map/reduce_scatter | solution.py:64
  144.6 1.9 copy.48
  149.7 44.8 %all-gather.6.cloned.1.call-done = bf16[1024,2,512]{0,2,1:T(8,128)(2,1)} async-done(((bf16[256,2,512]{0,2,1:T(8,128)(2,1)}), bf16[1024,2,512]{0,2,1:T(8,128)(2,1)}) %all-gather.6.cloned.1.call-update) | async-done | bytes 2097168 | tf_op jit(solution)/shard_map/all_gather | solution.py:225
  194.5 1.8 fusion.41
  196.4 1.8 fusion.45
  199.2 1.9 fusion.13
  201.1 28.5 %all-gather.8.cloned.1.call-done = bf16[1024,512]{0,1:T(8,128)(2,1)} async-done(((bf16[256,512]{0,1:T(8,128)(2,1)}), bf16[1024,512]{0,1:T(8,128)(2,1)}) %all-gather.8.cloned.1.call-update) | async-done | bytes 1048592 | tf_op jit(solution)/shard_map/all_gather | solution.py:75
  229.7 2.7 fusion.47
  232.4 10.4 all_gather.32
  243.6 5.8 fusion.50
  249.5 2.9 reduce-scatter.12.cloned.1.call-done
  253.7 10.6 all-reduce.3
  264.5 7.0 all_gather.30
  272.3 4.5 fusion.48
  276.9 121.6 %reduce-scatter.18.cloned.1.call-done = f32[256,2048]{1,0:T(8,128)} async-done(((f32[1024,2048]{1,0:T(8,128)}), f32[256,2048]{1,0:T(8,128)}) %reduce-scatter.18.cloned.1.call-update) | async-done | bytes 2097168 | tf_op jit(solution)/shard_map/reduce_scatter | solution.py:64
  398.5 147.5 %reduce-scatter.14.cloned.1.call-done = f32[256,2048]{1,0:T(8,128)} async-done(((f32[1024,2048]{1,0:T(8,128)}), f32[256,2048]{1,0:T(8,128)}) %reduce-scatter.14.cloned.1.call-update) | async-done | bytes 2097168 | tf_op jit(solution)/shard_map/reduce_scatter | solution.py:64
  546.0 3.7 fusion.7
  550.7 80.7 %all-gather.12.cloned.1.call-done = bf16[1024,2048]{1,0:T(8,128)(2,1)} async-done(((bf16[256,2048]{1,0:T(8,128)(2,1)}), bf16[1024,2048]{1,0:T(8,128)(2,1)}) %all-gather.12.cloned.1.call-update) | async-done | bytes 4194320 | tf_op jit(solution)/shard_map/all_gather | solution.py:75
  631.3 4.4 fusion.51
  635.9 77.0 %all-gather.10.cloned.1.call-done = bf16[1024,2048]{1,0:T(8,128)(2,1)} async-done(((bf16[256,2048]{1,0:T(8,128)(2,1)}), bf16[1024,2048]{1,0:T(8,128)(2,1)}) %all-gather.10.cloned.1.call-update) | async-done | bytes 4194320 | tf_op jit(solution)/shard_map/all_gather | solution.py:75
  712.9 4.7 fusion.49
  717.7 17.0 %reduce-scatter.20.cloned.1.call-done = f32[512,256]{1,0:T(8,128)} async-done(((f32[1024,256]{1,0:T(8,128)}), f32[512,256]{1,0:T(8,128)}) %reduce-scatter.20.cloned.1.call-update) | async-done | bytes 524304 | tf_op jit(solution)/shard_map/reduce_scatter | solution.py:82
  736.1 11.7 %all-reduce.2 = (f32[512]{0:T(512)S(1)}, f32[512]{0:T(512)S(1)}) all-reduce(f32[512]{0:T(512)S(1)} %get-tuple-element.124, f32[512]{0:T(512)S(1)} %get-tuple-element.128), channel_id=1, replica_groups=mesh['dp'=4,'row'=4,'col'=2] {'row'}, use_global_device_ids=true, to_apply=%region_21.22 | all-reduce | flops 1024 | bytes 8192 | tf_op jit(solution)/shard_map/psum | solution.py:23
  747.8 9.9 reduce-scatter.16.cloned.1.call-done
  757.7 2.4 fusion.39
  760.1 8.7 all_gather.34
  768.8 1.8 fusion.52
  770.7 44.0 %reduce-scatter.22.cloned.1.call-done = f32[256,512]{1,0:T(8,128)} async-done(((f32[1024,512]{1,0:T(8,128)}), f32[256,512]{1,0:T(8,128)}) %reduce-scatter.22.cloned.1.call-update) | async-done | bytes 524304 | tf_op jit(solution)/shard_map/reduce_scatter | solution.py:64
  815.8 3.3 fusion.8
  822.1 2.4 pad_maximum_fusion
  824.6 2.8 fusion.12
  827.4 73.4 %reduce-scatter.24.cloned.1.call-done = f32[256,2,512]{0,2,1:T(8,128)} async-done(((f32[1024,2,512]{0,2,1:T(8,128)}), f32[256,2,512]{0,2,1:T(8,128)}) %reduce-scatter.24.cloned.1.call-update) | async-done | bytes 1048592 | tf_op jit(solution)/shard_map/reduce_scatter | solution.py:254
  902.1 1.9 pad_maximum_fusion.1
  904.1 64.0 %all-gather.14.cloned.1.call-done = bf16[1024,1536]{0,1:T(8,128)(2,1)} async-done(((bf16[256,1536]{0,1:T(8,128)(2,1)}), bf16[1024,1536]{0,1:T(8,128)(2,1)}) %all-gather.14.cloned.1.call-update) | async-done | bytes 3145744 | tf_op jit(solution)/shard_map/all_gather | solution.py:75
  968.1 3.9 fusion.53
  972.3 4.9 fusion.55
  977.3 2.7 fusion.56
  981.2 2.1 fusion.57
  983.6 3.0 convert_reduce_fusion
  987.3 11.7 %all-reduce.5 = (f32[2,512]{1,0:T(2,128)}, f32[256]{0:T(256)}, f32[2048]{0:T(1024)}, f32[256]{0:T(256)}) all-reduce(f32[2,512]{1,0:T(2,128)S(1)} %pad_maximum_fusion.3, f32[256]{0:T(256)S(1)} %convert_reduce_fusion.3, f32[2048]{0:T(1024)S(1)} %convert_reduce_fusion, ...), channel_id=1, replica_groups=mesh['dp'=4,'row'=4,'col'=2] {'dp'}, use_global_device_ids=true, to_apply=%region_36.37 | all-reduce | flops 3584 | bytes 28672 | tf_op jit(solution)/shard_map/psum | solution.py:294
  1000.6 14.2 %all-reduce = (f32[256]{0:T(256)}, f32[256]{0:T(256)}, f32[256]{0:T(256)}, f32[256]{0:T(256)}) all-reduce(f32[256]{0:T(256)S(1)} %get-tuple-element.125, f32[256]{0:T(256)S(1)} %get-tuple-element.130, f32[256]{0:T(256)S(1)} %get-tuple-element.123, f32[256]{0:T(256)S(1)} %get-tuple-element.129), channel_id=1, replica_groups=mesh['dp'=4,'row'=4,'col'=2] {'dp','col'}, use_global_device_ids=true, to_apply=%region_31.32 | all-reduce | flops 1024 | bytes 8192 | tf_op jit(solution)/shard_map/psum | solution.py:313
  1014.8 8.9 all-reduce.1
  1023.7 2.2 fusion.24
  1025.9 88.7 %all-reduce.9.cloned.1.call-done = (f32[256,3,512]{0,2,1:T(8,128)}, f32[512,256]{1,0:T(8,128)}, f32[256,2048]{1,0:T(8,128)}, f32[2048,256]{1,0:T(8,128)}) async-done(((f32[256,3,512]{0,2,1:T(8,128)}, f32[512,256]{1,0:T(8,128)}, f32[256,2048]{1,0:T(8,128)}, f32[2048,256]{1,0:T(8,128)}), (f32[256,3,512]{0,2,1:T(8,128)}, f32[512,256]{1,0:T(8,128)}, f32[256,2048]{1,0:T(8,128)}, ...) | async-done | bytes 6291472 | tf_op jit(solution)/shard_map/psum | solution.py:294
  1114.6 3.2 copy.55
  (147 shorter events, 27.9 us)
Async XLA Ops:
  7.2 265.1 %copy-start = (bf16[256,2048]{1,0:T(8,128)(2,1)S(1)}, bf16[256,2048]{1,0:T(8,128)(2,1)}, u32[]{:S(2)}) copy-start(bf16[256,2048]{1,0:T(8,128)(2,1)} %param.28) | copy-start | bytes 3145732
  7.2 137.4 %reduce-scatter.10.cloned.1.call-start = ((), (), s32[]{:S(2)}) async-start(), calls=%async_computation.9 | async-start | bytes 7864320 | tf_op jit(solution)/shard_map/reduce_scatter | solution.py:64
  30.2 5.3 copy-start.9
  31.8 3.7 copy-start.13
  35.5 159.0 %all-gather.6.cloned.1.call-start = ((), (), s32[]{:S(2)}) async-start(), calls=%async_computation.10 | async-start | bytes 2621440 | tf_op jit(solution)/shard_map/all_gather | solution.py:225
  36.2 111.5 %copy-start.26 = (s32[1024]{0:T(1024)S(1)}, s32[1024]{0:T(1024)}, u32[]{:S(2)}) copy-start(s32[1024]{0:T(1024)} %param.19) | copy-start | bytes 12292
  36.2 111.7 %copy-start.35 = (s32[13]{0:T(128)S(1)}, s32[13]{0:T(128)}, u32[]{:S(2)}) copy-start(s32[13]{0:T(128)} %param.18) | copy-start | bytes 160
  146.7 49.7 %copy-start.19 = (f32[256,1,512]{0,2,1:T(8,128)}, f32[256,1,512]{0,2,1:T(8,128)S(1)}, u32[]{:S(2)}) copy-start(f32[256,1,512]{0,2,1:T(8,128)S(1)} %get-tuple-element.162) | copy-start | bytes 1572868
  147.6 82.1 %all-gather.8.cloned.1.call-start = ((), (), s32[]{:S(2)}) async-start(), calls=%async_computation.11 | async-start | bytes 1310720 | tf_op jit(solution)/shard_map/all_gather | solution.py:75
  194.5 1.9 copy-start.22
  196.3 1.8 copy-start.8
  198.1 2.9 copy-start.2
  199.2 30.5 %copy-start.24 = (bf16[512,256]{1,0:T(8,128)(2,1)S(1)}, bf16[512,256]{1,0:T(8,128)(2,1)}, u32[]{:S(2)}) copy-start(bf16[512,256]{1,0:T(8,128)(2,1)} %param.24) | copy-start | bytes 786436
  201.1 31.4 %copy-start.23 = (bf16[512,256]{1,0:T(8,128)(2,1)S(1)}, bf16[512,256]{1,0:T(8,128)(2,1)}, u32[]{:S(2)}) copy-start(bf16[512,256]{1,0:T(8,128)(2,1)} %param.17) | copy-start | bytes 786436
  201.1 51.3 %reduce-scatter.12.cloned.1.call-start = ((), (), s32[]{:S(2)}) async-start(), calls=%async_computation.12 | async-start | bytes 1572864 | tf_op jit(solution)/shard_map/reduce_scatter | solution.py:82
  232.4 166.1 %reduce-scatter.18.cloned.1.call-start = ((), (), s32[]{:S(2)}) async-start(), calls=%async_computation.16 | async-start | bytes 10485760 | tf_op jit(solution)/shard_map/reduce_scatter | solution.py:64
  249.4 3.0 copy-start.4
  249.4 3.0 copy-start.33
  249.4 14.9 %copy-start.27 = (f32[256]{0:T(256)S(1)}, f32[256]{0:T(256)}, u32[]{:S(2)}) copy-start(f32[256]{0:T(256)} %param.26) | copy-start | bytes 3076
  249.4 14.9 %copy-start.31 = (f32[256]{0:T(256)S(1)}, f32[256]{0:T(256)}, u32[]{:S(2)}) copy-start(f32[256]{0:T(256)} %param.27) | copy-start | bytes 3076
  249.4 296.6 %reduce-scatter.14.cloned.1.call-start = ((), (), s32[]{:S(2)}) async-start(), calls=%async_computation.13 | async-start | bytes 10485760 | tf_op jit(solution)/shard_map/reduce_scatter | solution.py:64
  276.8 269.2 %copy-start.29 = (f32[2048]{0:T(1024)S(1)}, f32[2048]{0:T(1024)}, u32[]{:S(2)}) copy-start(f32[2048]{0:T(1024)} %param.29) | copy-start | bytes 24580
  276.8 354.5 %all-gather.12.cloned.1.call-start = ((), (), s32[]{:S(2)}) async-start(), calls=%async_computation.17 | async-start | bytes 5242880 | tf_op jit(solution)/shard_map/all_gather | solution.py:75
  549.7 163.2 %all-gather.10.cloned.1.call-start = ((), (), s32[]{:S(2)}) async-start(), calls=%async_computation.14 | async-start | bytes 5242880 | tf_op jit(solution)/shard_map/all_gather | solution.py:75
  550.5 184.2 %reduce-scatter.20.cloned.1.call-start = ((), (), s32[]{:S(2)}) async-start(), calls=%async_computation.18 | async-start | bytes 1572864 | tf_op jit(solution)/shard_map/reduce_scatter | solution.py:82
  635.8 121.9 %copy-start.32 = (f32[256]{0:T(256)S(1)}, f32[256]{0:T(256)}, u32[]{:S(2)}) copy-start(f32[256]{0:T(256)} %param.31) | copy-start | bytes 3076
  635.8 121.9 %reduce-scatter.16.cloned.1.call-start = ((), (), s32[]{:S(2)}) async-start(), calls=%async_computation.15 | async-start | bytes 1572864 | tf_op jit(solution)/shard_map/reduce_scatter | solution.py:82
  717.6 97.0 %reduce-scatter.22.cloned.1.call-start = ((), (), s32[]{:S(2)}) async-start(), calls=%async_computation.19 | async-start | bytes 2621440 | tf_op jit(solution)/shard_map/reduce_scatter | solution.py:64
  770.6 130.2 %reduce-scatter.24.cloned.1.call-start = ((), (), s32[]{:S(2)}) async-start(), calls=%async_computation.20 | async-start | bytes 5242880 | tf_op jit(solution)/shard_map/reduce_scatter | solution.py:254
  815.8 3.5 copy-start.3
  820.6 1.0 copy-start.20
  824.6 143.5 %all-gather.14.cloned.1.call-start = ((), (), s32[]{:S(2)}) async-start(), calls=%async_computation.21 | async-start | bytes 3932160 | tf_op jit(solution)/shard_map/all_gather | solution.py:75
  827.4 140.7 %copy-start.14 = (bf16[256,3,512]{0,2,1:T(8,128)(2,1)S(1)}, bf16[256,3,512]{0,2,1:T(8,128)(2,1)}, u32[]{:S(2)}) copy-start(bf16[256,3,512]{0,2,1:T(8,128)(2,1)} %copy-done.13) | copy-start | bytes 2359300
  904.0 68.3 %copy-start.16 = (bf16[1024,256]{1,0:T(8,128)(2,1)S(1)}, bf16[1024,256]{1,0:T(8,128)(2,1)}, u32[]{:S(2)}) copy-start(bf16[1024,256]{1,0:T(8,128)(2,1)} %copy-done.15) | copy-start | bytes 1572868
  904.0 95.0 %reduce-scatter.26.cloned.1.call-start = ((), (), s32[]{:S(2)}) async-start(), calls=%async_computation.22 | async-start | bytes 1572864 | tf_op jit(solution)/shard_map/reduce_scatter | solution.py:82
  972.0 5.2 copy-start.6
  972.0 142.6 %all-reduce.9.cloned.1.call-start = ((), (), s32[]{:S(2)}) async-start(), calls=%async_computation.23 | async-start | bytes 12582912 | tf_op jit(solution)/shard_map/psum | solution.py:294
  972.3 4.9 copy-start.34
  977.3 2.7 copy-start.7
  977.3 4.0 copy-start.10
  977.3 4.0 copy-start.11
  983.4 3.4 copy-start.12
  983.6 15.4 %copy-start.28 = (f32[256]{0:T(256)S(1)}, f32[256]{0:T(256)}, u32[]{:S(2)}) copy-start(f32[256]{0:T(256)} %param.20) | copy-start | bytes 3076
  986.6 37.1 %copy-start.21 = (f32[512,256]{1,0:T(8,128)S(1)}, f32[512,256]{1,0:T(8,128)}, u32[]{:S(2)}) copy-start(f32[512,256]{1,0:T(8,128)} %get-tuple-element.156) | copy-start | bytes 1572868
  1114.6 3.2 copy-start.25
  1114.6 4.0 copy-start.18
  1117.8 2.1 copy-start.17
  1118.6 2.6 copy-start.1
  (3 other events, 2.3 us)
Sparse Core Ops, SparseCore 0:
  35.6 108.9 reduce-scatter.9
  147.7 46.7 all-gather.5
  201.2 28.4 all-gather.7
  232.5 19.8 reduce-scatter.11
  254.7 143.6 reduce-scatter.17
  400.8 145.1 reduce-scatter.13
  549.8 81.4 all-gather.11
  633.6 79.2 all-gather.9
  715.8 18.8 reduce-scatter.19
  737.3 20.3 reduce-scatter.15
  770.7 43.8 reduce-scatter.21
  824.7 76.0 reduce-scatter.23
  904.1 63.9 all-gather.13
  972.2 18.4 reduce-scatter.25
  994.3 120.2 all-reduce.8
where the time goes:
time: 1130 us
  waiting for transfers between devices  909 us (80%)
  blocking collectives  104 us (9%)
  matrix products  53.8 us (5%)
  other arithmetic  30.3 us (3%)
  local copies, waits for them, and re-layouts  15.1 us (1%)
  between operations  14.3 us (1%)
    reduce_scatter x4, waiting for transfers between devices, across_rows(): lax.psum_scatter(partial_term(jnp.int32(0), row_count * lax.axis_size('ro...  422 us
    all_gather x4, waiting for transfers between devices, across_cols(): gathered = lax.all_gather(operand, 'row', axis=0, tiled=True)  250 us
    psum x1, waiting for transfers between devices, on_device(): lax.psum((weight_terms[0], weight_terms[1], weight_terms[2], weight_terms...  88.7 us
    reduce_scatter x1, waiting for transfers between devices, on_device(): lax.psum_scatter(jnp.stack([key_grad.reshape(-1, col_width), value_grad.r...  73.4 us
    all_gather x1, waiting for transfers between devices, on_device(): lax.all_gather(jnp.stack([keys_here, values_here], axis=1), 'row', axis=0...  44.8 us
    psum x4, blocking collectives, width_sums(): lax.psum((jnp.sum(first_term, axis=1), jnp.sum(second_term, axis=1)), 'row')  44.6 us
    all_gather x4, blocking collectives, across_rows(): gathered = lax.all_gather(operand, 'col', axis=0, tiled=True)  33.2 us
    reduce_scatter x4, waiting for transfers between devices, across_cols(): lax.psum_scatter(partial_term(jnp.int32(0), row_count * lax.axis_size('co...  29.8 us
  transfers between devices with their start and end apart: 15, of which 14 were waited for; matrix products, arithmetic and copies ran while one was open for 4% of the time, Pallas kernels for 0%

commit v1 on v0

--- a/solution.py
+++ b/solution.py
@@ -72,7 +72,12 @@
 
 
 def across_cols(operand, weight_block, flipped):
-    gathered = lax.all_gather(operand, "row", axis=0, tiled=True)
+    ring = [operand]
+    for hop in range(3):
+        ring.append(lax.ppermute(ring[-1], "row", [(dev, (dev + 1) % 4) for dev in range(4)]))
+    gathered = jnp.roll(
+        jnp.concatenate(ring[::-1], axis=0), (lax.axis_index("row") + 1) * ring[0].shape[0], axis=0
+    )
     row_count = gathered.shape[0] // lax.axis_size("col")
 
     def partial_term(row_start, row_num):

time: 1130 us -> 1120 us (level)
  waiting for transfers between devices: 909 us -> 844 us
  other arithmetic: 30.3 us -> 63.4 us
  local copies, waits for them, and re-layouts: 15.1 us -> 28.6 us
    all_gather x4 -> x0, waiting for transfers between devices: 250 us -> none  [across_cols(): gathered = lax.all_gather(operand, 'row', axis=0, tiled=True)]
    ppermute x0 -> x12, waiting for transfers between devices: none -> 199 us  [across_cols(): lax.ppermute(ring[-1], 'row', [(dev, (dev + 1) % 4) for dev in range(4)])]
    reduce_sum x1, other arithmetic: 3.02 us -> 23.6 us  [on_device(): jnp.sum(pre_all.astype(jnp.float32), axis=0)]
    reduce_scatter x4, waiting for transfers between devices: 29.8 us -> 14.6 us  [across_cols(): lax.psum_scatter(partial_term(jnp.int32(0), row_count * lax.axis_size('co...]
    concatenate x0 -> x1, other arithmetic: none -> 13.5 us  [across_cols(): jnp.roll(jnp.concatenate(ring[::-1], axis=0), (lax.axis_index('row') + 1)...]
    unnamed x77 -> x101, local copies, waits for them, and re-layouts: 10.9 us -> 24.4 us
  transfers between devices with their start and end apart: 15 -> 23, of which waited for: 14 -> 21; matrix products, arithmetic and copies ran while one was open for 4% -> 7% of each run, Pallas kernels for 0% -> 0%
where the time goes in v1:
time: 1120 us; the launch traced here: 1110 us
  waiting for transfers between devices  844 us (75%)
  blocking collectives  105 us (9%)
  other arithmetic  63.4 us (6%)
  matrix products  45 us (4%)
  local copies, waits for them, and re-layouts  28.6 us (3%)
  between operations  14.7 us (1%)
    reduce_scatter x4, waiting for transfers between devices, across_rows(): lax.psum_scatter(partial_term(jnp.int32(0), row_count * lax.axis_size('ro...  421 us
    ppermute x12, waiting for transfers between devices, across_cols(): lax.ppermute(ring[-1], 'row', [(dev, (dev + 1) % 4) for dev in range(4)])  199 us
    psum x1, waiting for transfers between devices, on_device(): lax.psum((weight_terms[0], weight_terms[1], weight_terms[2], weight_terms...  91 us
    reduce_scatter x1, waiting for transfers between devices, on_device(): lax.psum_scatter(jnp.stack([key_grad.reshape(-1, col_width), value_grad.r...  73.2 us
    all_gather x1, waiting for transfers between devices, on_device(): lax.all_gather(jnp.stack([keys_here, values_here], axis=1), 'row', axis=0...  45.8 us
    psum x4, blocking collectives, width_sums(): lax.psum((jnp.sum(first_term, axis=1), jnp.sum(second_term, axis=1)), 'row')  45.2 us
    all_gather x4, blocking collectives, across_rows(): gathered = lax.all_gather(operand, 'col', axis=0, tiled=True)  35 us
    unnamed x101, local copies, waits for them, and re-layouts  24.4 us
  transfers between devices with their start and end apart: 23, of which 21 were waited for; matrix products, arithmetic and copies ran while one was open for 7% of the time, Pallas kernels for 0%

profile of v1, /device:TPU:0, one launch (start us, length us, event | category | flops | bytes accessed | tf_op | source)
XLA Modules:
  0.0 1107.7 jit_solution(11871256982260891722)
XLA Ops:
  8.5 13.5 %all-reduce.4 = (f32[512]{0:T(512)S(1)}, f32[512]{0:T(512)S(1)}) all-reduce(f32[512]{0:T(512)S(1)} %get-tuple-element.135, f32[512]{0:T(512)S(1)} %get-tuple-element.134), channel_id=1, replica_groups=mesh['dp'=4,'row'=4,'col'=2] {'row'}, use_global_device_ids=true, to_apply=%region_3.4 | all-reduce | flops 1024 | bytes 8192 | tf_op jit(solution)/shard_map/psum | solution.py:23
  23.1 7.0 all_gather.15
  31.8 3.7 fusion.73
  36.2 108.4 %reduce-scatter.10.cloned.1.call-done = f32[256,1536]{1,0:T(8,128)} async-done(((f32[1024,1536]{1,0:T(8,128)}), f32[256,1536]{1,0:T(8,128)}) %reduce-scatter.10.cloned.1.call-update) | async-done | bytes 1572880 | tf_op jit(solution)/shard_map/reduce_scatter | solution.py:64
  148.8 45.8 %all-gather.2.cloned.1.call-done = bf16[1024,2,512]{0,2,1:T(8,128)(2,1)} async-done(((bf16[256,2,512]{0,2,1:T(8,128)(2,1)}), bf16[1024,2,512]{0,2,1:T(8,128)(2,1)}) %all-gather.2.cloned.1.call-update) | async-done | bytes 2097168 | tf_op jit(solution)/shard_map/all_gather | solution.py:230
  201.5 9.0 collective-permute-done
  210.5 8.2 collective-permute-done.1
  218.7 8.2 collective-permute-done.2
  228.5 2.4 fusion.34
  231.0 12.2 %all_gather.18 = bf16[1024,256]{1,0:T(8,128)(2,1)S(1)} all-gather(bf16[512,256]{1,0:T(8,128)(2,1)S(1)} %copy-done.30), channel_id=1, replica_groups=mesh['dp'=4,'row'=4,'col'=2] {'col'}, dimensions={0}, use_global_device_ids=true | all-gather | bytes 786432 | tf_op jit(solution)/shard_map/all_gather | solution.py:57
  244.0 4.5 fusion.76
  248.6 3.3 reduce-scatter.12.cloned.1.call-done
  253.1 11.6 %all-reduce.3 = (f32[512]{0:T(512)S(1)}, f32[512]{0:T(512)S(1)}) all-reduce(f32[512]{0:T(512)S(1)} %get-tuple-element.133, f32[512]{0:T(512)S(1)} %get-tuple-element.132), channel_id=1, replica_groups=mesh['dp'=4,'row'=4,'col'=2] {'row'}, use_global_device_ids=true, to_apply=%region_13.14 | all-reduce | flops 1024 | bytes 8192 | tf_op jit(solution)/shard_map/psum | solution.py:23
  264.9 7.0 all_gather.17
  272.8 4.5 fusion.74
  277.8 120.7 %reduce-scatter.18.cloned.1.call-done = f32[256,2048]{1,0:T(8,128)} async-done(((f32[1024,2048]{1,0:T(8,128)}), f32[256,2048]{1,0:T(8,128)}) %reduce-scatter.18.cloned.1.call-update) | async-done | bytes 2097168 | tf_op jit(solution)/shard_map/reduce_scatter | solution.py:64
  398.5 147.5 %reduce-scatter.14.cloned.1.call-done = f32[256,2048]{1,0:T(8,128)} async-done(((f32[1024,2048]{1,0:T(8,128)}), f32[256,2048]{1,0:T(8,128)}) %reduce-scatter.14.cloned.1.call-update) | async-done | bytes 2097168 | tf_op jit(solution)/shard_map/reduce_scatter | solution.py:64
  545.9 2.7 fusion.25
  549.9 2.5 collective-permute-start.3
  552.4 24.2 %collective-permute-done.6 = bf16[256,2048]{1,0:T(8,128)(2,1)S(1)} collective-permute-done((bf16[256,2048]{1,0:T(8,128)(2,1)S(1)}, bf16[256,2048]{1,0:T(8,128)(2,1)S(1)}, u32[]{:S(2)}, u32[]{:S(2)}) %collective-permute-start.6) | collective-permute-done | bytes 1048608 | tf_op jit(solution)/shard_map/ppermute | solution.py:77
  576.6 22.5 %collective-permute-done.3 = bf16[256,2048]{1,0:T(8,128)(2,1)S(1)} collective-permute-done((bf16[256,2048]{1,0:T(8,128)(2,1)S(1)}, bf16[256,2048]{1,0:T(8,128)(2,1)S(1)}, u32[]{:S(2)}, u32[]{:S(2)}) %collective-permute-start.3) | collective-permute-done | bytes 1048608 | tf_op jit(solution)/shard_map/ppermute | solution.py:77
  599.1 22.5 %collective-permute-done.7 = bf16[256,2048]{1,0:T(8,128)(2,1)S(1)} collective-permute-done((bf16[256,2048]{1,0:T(8,128)(2,1)S(1)}, bf16[256,2048]{1,0:T(8,128)(2,1)S(1)}, u32[]{:S(2)}, u32[]{:S(2)}) %collective-permute-start.7) | collective-permute-done | bytes 1048608 | tf_op jit(solution)/shard_map/ppermute | solution.py:77
  621.5 22.6 %collective-permute-done.4 = bf16[256,2048]{1,0:T(8,128)(2,1)} collective-permute-done((bf16[256,2048]{1,0:T(8,128)(2,1)S(1)}, bf16[256,2048]{1,0:T(8,128)(2,1)}, u32[]{:S(2)}, u32[]{:S(2)}) %collective-permute-start.4) | collective-permute-done | bytes 1048608 | tf_op jit(solution)/shard_map/ppermute | solution.py:77
  644.1 22.4 %collective-permute-done.8 = bf16[256,2048]{1,0:T(8,128)(2,1)S(1)} collective-permute-done((bf16[256,2048]{1,0:T(8,128)(2,1)S(1)}, bf16[256,2048]{1,0:T(8,128)(2,1)S(1)}, u32[]{:S(2)}, u32[]{:S(2)}) %collective-permute-start.8) | collective-permute-done | bytes 1048608 | tf_op jit(solution)/shard_map/ppermute | solution.py:77
  666.5 23.6 %convert_reduce_fusion = (f32[2048]{0:T(1024)S(1)}, bf16[1024,2048]{1,0:T(8,128)(2,1)S(1)}) fusion(s32[]{:T(128)S(6)} %select_n.105, bf16[256,2048]{1,0:T(8,128)(2,1)S(1)} %get-tuple-element.161, bf16[256,2048]{1,0:T(8,128)(2,1)S(1)} %collective-permute-done.6, bf16[256,2048]{1,0:T(8,128)(2,1)S(1)} %collective-permute-done.7, ...), kind=kLoop, calls=%fused_computation.16 | loop fusion | flops 37746688 | bytes 8396804 | tf_op jit(solution)/shard_map/reduce_sum | solution.py:286
  694.7 13.5 %fusion.10 = bf16[1024,2048]{1,0:T(8,128)(2,1)S(1)} fusion(s32[]{:T(128)S(6)} %select_n.105, bf16[256,2048]{1,0:T(8,128)(2,1)} %collective-permute-done.5, bf16[256,2048]{1,0:T(8,128)(2,1)} %collective-permute-done.4, bf16[256,2048]{1,0:T(8,128)(2,1)} %copy-done.29, bf16[256,2048]{1,0:T(8,128)(2,1)S(1)} %get-tuple-element.162), kind=kLoop, calls=%fused_computation.28 | loop fusion | flops 33554432 | bytes 8388612 | tf_op jit(solution)/shard_map/jit(_roll_dynamic)/concatenate | solution.py:78
  715.2 11.7 %all-reduce.2 = (f32[512]{0:T(512)S(1)}, f32[512]{0:T(512)S(1)}) all-reduce(f32[512]{0:T(512)S(1)} %get-tuple-element.125, f32[512]{0:T(512)S(1)} %get-tuple-element.129), channel_id=1, replica_groups=mesh['dp'=4,'row'=4,'col'=2] {'row'}, use_global_device_ids=true, to_apply=%region_21.23 | all-reduce | flops 1024 | bytes 8192 | tf_op jit(solution)/shard_map/psum | solution.py:23
  726.9 10.0 reduce-scatter.16.cloned.1.call-done
  736.9 2.4 fusion.66
  739.4 8.7 all_gather.19
  750.0 44.0 %reduce-scatter.22.cloned.1.call-done = f32[256,512]{1,0:T(8,128)} async-done(((f32[1024,512]{1,0:T(8,128)}), f32[256,512]{1,0:T(8,128)}) %reduce-scatter.22.cloned.1.call-update) | async-done | bytes 524304 | tf_op jit(solution)/shard_map/reduce_scatter | solution.py:64
  795.2 3.2 fusion.26
  801.5 2.4 pad_maximum_fusion
  804.1 2.8 fusion.30
  806.9 73.2 %reduce-scatter.24.cloned.1.call-done = f32[256,2,512]{0,2,1:T(8,128)} async-done(((f32[1024,2,512]{0,2,1:T(8,128)}), f32[256,2,512]{0,2,1:T(8,128)}) %reduce-scatter.24.cloned.1.call-update) | async-done | bytes 1048592 | tf_op jit(solution)/shard_map/reduce_scatter | solution.py:259
  883.9 19.6 %collective-permute-done.9 = bf16[256,1536]{0,1:T(8,128)(2,1)S(1)} collective-permute-done((bf16[256,1536]{0,1:T(8,128)(2,1)S(1)}, bf16[256,1536]{0,1:T(8,128)(2,1)S(1)}, u32[]{:S(2)}, u32[]{:S(2)}) %collective-permute-start.9) | collective-permute-done | bytes 786464 | tf_op jit(solution)/shard_map/ppermute | solution.py:77
  903.5 20.3 %collective-permute-done.10 = bf16[256,1536]{0,1:T(8,128)(2,1)S(1)} collective-permute-done((bf16[256,1536]{0,1:T(8,128)(2,1)S(1)}, bf16[256,1536]{0,1:T(8,128)(2,1)S(1)}, u32[]{:S(2)}, u32[]{:S(2)}) %collective-permute-start.10) | collective-permute-done | bytes 786464 | tf_op jit(solution)/shard_map/ppermute | solution.py:77
  923.8 19.3 %collective-permute-done.11 = bf16[256,1536]{0,1:T(8,128)(2,1)S(1)} collective-permute-done((bf16[256,1536]{0,1:T(8,128)(2,1)S(1)}, bf16[256,1536]{0,1:T(8,128)(2,1)S(1)}, u32[]{:S(2)}, u32[]{:S(2)}) %collective-permute-start.11) | collective-permute-done | bytes 786464 | tf_op jit(solution)/shard_map/ppermute | solution.py:77
  944.1 2.7 copy-done.21
  948.8 4.9 fusion.79
  953.8 2.7 fusion.80
  960.8 2.4 convert_reduce_fusion.1
  963.2 10.7 all-reduce.5
  975.4 14.3 %all-reduce = (f32[256]{0:T(256)}, f32[256]{0:T(256)}, f32[256]{0:T(256)}, f32[256]{0:T(256)}) all-reduce(f32[256]{0:T(256)S(1)} %get-tuple-element.126, f32[256]{0:T(256)S(1)} %get-tuple-element.131, f32[256]{0:T(256)S(1)} %get-tuple-element.124, f32[256]{0:T(256)S(1)} %get-tuple-element.130), channel_id=1, replica_groups=mesh['dp'=4,'row'=4,'col'=2] {'dp','col'}, use_global_device_ids=true, to_apply=%region_31.33 | all-reduce | flops 1024 | bytes 8192 | tf_op jit(solution)/shard_map/psum | solution.py:318
  989.7 8.5 all-reduce.1
  1000.4 91.0 %all-reduce.9.cloned.1.call-done = (f32[256,3,512]{0,2,1:T(8,128)}, f32[512,256]{1,0:T(8,128)}, f32[256,2048]{1,0:T(8,128)}, f32[2048,256]{1,0:T(8,128)}) async-done(((f32[256,3,512]{0,2,1:T(8,128)}, f32[512,256]{1,0:T(8,128)}, f32[256,2048]{1,0:T(8,128)}, f32[2048,256]{1,0:T(8,128)}), (f32[256,3,512]{0,2,1:T(8,128)}, f32[512,256]{1,0:T(8,128)}, f32[256,2048]{1,0:T(8,128)}, ...) | async-done | bytes 6291472 | tf_op jit(solution)/shard_map/psum | solution.py:299
  1091.4 3.2 copy.55
  1096.5 3.1 copy.80
  (186 shorter events, 58.0 us)
Async XLA Ops:
  7.2 265.6 %copy-start = (bf16[256,2048]{1,0:T(8,128)(2,1)S(1)}, bf16[256,2048]{1,0:T(8,128)(2,1)}, u32[]{:S(2)}) copy-start(bf16[256,2048]{1,0:T(8,128)(2,1)} %param.30) | copy-start | bytes 3145732
  7.2 137.4 %reduce-scatter.10.cloned.1.call-start = ((), (), s32[]{:S(2)}) async-start(), calls=%async_computation.9 | async-start | bytes 7864320 | tf_op jit(solution)/shard_map/reduce_scatter | solution.py:64
  30.2 5.3 copy-start.13
  31.8 3.7 copy-start.15
  35.5 112.2 %copy-start.32 = (s32[1024]{0:T(1024)S(1)}, s32[1024]{0:T(1024)}, u32[]{:S(2)}) copy-start(s32[1024]{0:T(1024)} %param.21) | copy-start | bytes 12292
  35.5 112.4 %copy-start.40 = (s32[13]{0:T(128)S(1)}, s32[13]{0:T(128)}, u32[]{:S(2)}) copy-start(s32[13]{0:T(128)} %param.20) | copy-start | bytes 160
  35.5 159.0 %all-gather.2.cloned.1.call-start = ((), (), s32[]{:S(2)}) async-start(), calls=%async_computation.10 | async-start | bytes 2621440 | tf_op jit(solution)/shard_map/all_gather | solution.py:230
  146.7 52.3 %copy-start.24 = (f32[256,1,512]{0,2,1:T(8,128)}, f32[256,1,512]{0,2,1:T(8,128)S(1)}, u32[]{:S(2)}) copy-start(f32[256,1,512]{0,2,1:T(8,128)S(1)} %get-tuple-element.165) | copy-start | bytes 1572868
  147.6 104.2 %reduce-scatter.12.cloned.1.call-start = ((), (), s32[]{:S(2)}) async-start(), calls=%async_computation.11 | async-start | bytes 1572864 | tf_op jit(solution)/shard_map/reduce_scatter | solution.py:87
  196.3 3.8 copy-start.11
  201.2 29.7 %copy-start.30 = (bf16[512,256]{1,0:T(8,128)(2,1)S(1)}, bf16[512,256]{1,0:T(8,128)(2,1)}, u32[]{:S(2)}) copy-start(bf16[512,256]{1,0:T(8,128)(2,1)} %param.19) | copy-start | bytes 786436
  201.2 9.2 collective-permute-start
  210.5 8.2 collective-permute-start.1
  218.7 8.2 collective-permute-start.2
  218.7 25.3 %copy-start.27 = (bf16[2048,256]{1,0:T(8,128)(2,1)S(1)}, bf16[2048,256]{1,0:T(8,128)(2,1)}, u32[]{:S(2)}) copy-start(bf16[2048,256]{1,0:T(8,128)(2,1)} %param.32) | copy-start | bytes 3145732
  230.9 167.6 %reduce-scatter.18.cloned.1.call-start = ((), (), s32[]{:S(2)}) async-start(), calls=%async_computation.14 | async-start | bytes 10485760 | tf_op jit(solution)/shard_map/reduce_scatter | solution.py:64
  248.5 16.2 %copy-start.33 = (f32[256]{0:T(256)S(1)}, f32[256]{0:T(256)}, u32[]{:S(2)}) copy-start(f32[256]{0:T(256)} %param.28) | copy-start | bytes 3076
  248.5 16.2 %copy-start.37 = (f32[256]{0:T(256)S(1)}, f32[256]{0:T(256)}, u32[]{:S(2)}) copy-start(f32[256]{0:T(256)} %param.29) | copy-start | bytes 3076
  248.5 297.4 %reduce-scatter.14.cloned.1.call-start = ((), (), s32[]{:S(2)}) async-start(), calls=%async_computation.12 | async-start | bytes 10485760 | tf_op jit(solution)/shard_map/reduce_scatter | solution.py:64
  277.2 268.7 %copy-start.35 = (f32[2048]{0:T(1024)S(1)}, f32[2048]{0:T(1024)}, u32[]{:S(2)}) copy-start(f32[2048]{0:T(1024)} %param.31) | copy-start | bytes 24580
  277.3 436.5 %reduce-scatter.20.cloned.1.call-start = ((), (), s32[]{:S(2)}) async-start(), calls=%async_computation.15 | async-start | bytes 1572864 | tf_op jit(solution)/shard_map/reduce_scatter | solution.py:87
  548.7 27.9 %collective-permute-start.6 = (bf16[256,2048]{1,0:T(8,128)(2,1)S(1)}, bf16[256,2048]{1,0:T(8,128)(2,1)S(1)}, u32[]{:S(2)}, u32[]{:S(2)}) collective-permute-start(bf16[256,2048]{1,0:T(8,128)(2,1)S(1)} %get-tuple-element.161), channel_id=1, source_target_pairs={{0,2},{2,4},{4,6},{6,0},{1,3},{3,5},{5,7},{7,1},{8,10},{10,12},{12... | collective-permute-start | bytes 3145736 | tf_op jit(solution)/shard_map/ppermute | solution.py:77
  549.9 49.2 %collective-permute-start.3 = (bf16[256,2048]{1,0:T(8,128)(2,1)S(1)}, bf16[256,2048]{1,0:T(8,128)(2,1)S(1)}, u32[]{:S(2)}, u32[]{:S(2)}) collective-permute-start(bf16[256,2048]{1,0:T(8,128)(2,1)S(1)} %get-tuple-element.162), channel_id=1, source_target_pairs={{0,2},{2,4},{4,6},{6,0},{1,3},{3,5},{5,7},{7,1},{8,10},{10,12},{12... | collective-permute-start | bytes 3145736 | tf_op jit(solution)/shard_map/ppermute | solution.py:77
  576.6 44.9 %collective-permute-start.7 = (bf16[256,2048]{1,0:T(8,128)(2,1)S(1)}, bf16[256,2048]{1,0:T(8,128)(2,1)S(1)}, u32[]{:S(2)}, u32[]{:S(2)}) collective-permute-start(bf16[256,2048]{1,0:T(8,128)(2,1)S(1)} %collective-permute-done.6), channel_id=1, source_target_pairs={{0,2},{2,4},{4,6},{6,0},{1,3},{3,5},{5,7},{7,1},{8,10},{10,12},{12... | collective-permute-start | bytes 3145736 | tf_op jit(solution)/shard_map/ppermute | solution.py:77
  599.1 45.1 %copy-start.29 = (bf16[256,2048]{1,0:T(8,128)(2,1)}, bf16[256,2048]{1,0:T(8,128)(2,1)S(1)}, u32[]{:S(2)}) copy-start(bf16[256,2048]{1,0:T(8,128)(2,1)S(1)} %collective-permute-done.3) | copy-start | bytes 3145732
  599.1 45.0 %collective-permute-start.4 = (bf16[256,2048]{1,0:T(8,128)(2,1)S(1)}, bf16[256,2048]{1,0:T(8,128)(2,1)}, u32[]{:S(2)}, u32[]{:S(2)}) collective-permute-start(bf16[256,2048]{1,0:T(8,128)(2,1)S(1)} %collective-permute-done.3), channel_id=1, source_target_pairs={{0,2},{2,4},{4,6},{6,0},{1,3},{3,5},{5,7},{7,1},{8,10},{10,12},{12... | collective-permute-start | bytes 3145736 | tf_op jit(solution)/shard_map/ppermute | solution.py:77
  621.5 44.9 %collective-permute-start.8 = (bf16[256,2048]{1,0:T(8,128)(2,1)S(1)}, bf16[256,2048]{1,0:T(8,128)(2,1)S(1)}, u32[]{:S(2)}, u32[]{:S(2)}) collective-permute-start(bf16[256,2048]{1,0:T(8,128)(2,1)S(1)} %collective-permute-done.7), channel_id=1, source_target_pairs={{0,2},{2,4},{4,6},{6,0},{1,3},{3,5},{5,7},{7,1},{8,10},{10,12},{12... | collective-permute-start | bytes 3145736 | tf_op jit(solution)/shard_map/ppermute | solution.py:77
  644.1 50.6 %collective-permute-start.5 = (bf16[256,2048]{1,0:T(8,128)(2,1)}, bf16[256,2048]{1,0:T(8,128)(2,1)}, u32[]{:S(2)}, u32[]{:S(2)}) collective-permute-start(bf16[256,2048]{1,0:T(8,128)(2,1)} %collective-permute-done.4), channel_id=1, source_target_pairs={{0,2},{2,4},{4,6},{6,0},{1,3},{3,5},{5,7},{7,1},{8,10},{10,12},{12... | collective-permute-start | bytes 3145736 | tf_op jit(solution)/shard_map/ppermute | solution.py:77
  694.4 15.9 %copy-start.28 = (bf16[2048,256]{1,0:T(8,128)(2,1)S(1)}, bf16[2048,256]{1,0:T(8,128)(2,1)}, u32[]{:S(2)}) copy-start(bf16[2048,256]{1,0:T(8,128)(2,1)} %param.32) | copy-start | bytes 3145732
  694.4 42.5 %reduce-scatter.16.cloned.1.call-start = ((), (), s32[]{:S(2)}) async-start(), calls=%async_computation.13 | async-start | bytes 1572864 | tf_op jit(solution)/shard_map/reduce_scatter | solution.py:87
  710.3 26.7 %copy-start.38 = (f32[256]{0:T(256)S(1)}, f32[256]{0:T(256)}, u32[]{:S(2)}) copy-start(f32[256]{0:T(256)} %param.33) | copy-start | bytes 3076
  712.5 35.6 %copy-start.31 = (bf16[512,256]{1,0:T(8,128)(2,1)S(1)}, bf16[512,256]{1,0:T(8,128)(2,1)}, u32[]{:S(2)}) copy-start(bf16[512,256]{1,0:T(8,128)(2,1)} %param.26) | copy-start | bytes 786436
  712.5 81.4 %reduce-scatter.22.cloned.1.call-start = ((), (), s32[]{:S(2)}) async-start(), calls=%async_computation.16 | async-start | bytes 2621440 | tf_op jit(solution)/shard_map/reduce_scatter | solution.py:64
  749.9 48.5 %copy-start.12 = (bf16[1024,1,512]{0,2,1:T(8,128)(2,1)S(1)}, bf16[1024,1,512]{0,2,1:T(8,128)(2,1)}, u32[]{:S(2)}) copy-start(bf16[1024,1,512]{0,2,1:T(8,128)(2,1)} %copy-done.11) | copy-start | bytes 3145732
  749.9 130.1 %reduce-scatter.24.cloned.1.call-start = ((), (), s32[]{:S(2)}) async-start(), calls=%async_computation.17 | async-start | bytes 5242880 | tf_op jit(solution)/shard_map/reduce_scatter | solution.py:259
  803.8 170.1 %reduce-scatter.26.cloned.1.call-start = ((), (), s32[]{:S(2)}) async-start(), calls=%async_computation.18 | async-start | bytes 1572864 | tf_op jit(solution)/shard_map/reduce_scatter | solution.py:87
  882.4 21.2 %collective-permute-start.9 = (bf16[256,1536]{0,1:T(8,128)(2,1)S(1)}, bf16[256,1536]{0,1:T(8,128)(2,1)S(1)}, u32[]{:S(2)}, u32[]{:S(2)}) collective-permute-start(bf16[256,1536]{0,1:T(8,128)(2,1)S(1)} %bitcast.54), channel_id=1, source_target_pairs={{0,2},{2,4},{4,6},{6,0},{1,3},{3,5},{5,7},{7,1},{8,10},{10,12},{12... | collective-permute-start | bytes 2359304 | tf_op jit(solution)/shard_map/ppermute | solution.py:77
  903.5 20.3 %collective-permute-start.10 = (bf16[256,1536]{0,1:T(8,128)(2,1)S(1)}, bf16[256,1536]{0,1:T(8,128)(2,1)S(1)}, u32[]{:S(2)}, u32[]{:S(2)}) collective-permute-start(bf16[256,1536]{0,1:T(8,128)(2,1)S(1)} %collective-permute-done.9), channel_id=1, source_target_pairs={{0,2},{2,4},{4,6},{6,0},{1,3},{3,5},{5,7},{7,1},{8,10},{10,12},{12... | collective-permute-start | bytes 2359304 | tf_op jit(solution)/shard_map/ppermute | solution.py:77
  923.8 19.3 %collective-permute-start.11 = (bf16[256,1536]{0,1:T(8,128)(2,1)S(1)}, bf16[256,1536]{0,1:T(8,128)(2,1)S(1)}, u32[]{:S(2)}, u32[]{:S(2)}) collective-permute-start(bf16[256,1536]{0,1:T(8,128)(2,1)S(1)} %collective-permute-done.10), channel_id=1, source_target_pairs={{0,2},{2,4},{4,6},{6,0},{1,3},{3,5},{5,7},{7,1},{8,10},{10,12},{12... | collective-permute-start | bytes 2359304 | tf_op jit(solution)/shard_map/ppermute | solution.py:77
  948.7 5.0 copy-start.6
  948.8 142.6 %all-reduce.9.cloned.1.call-start = ((), (), s32[]{:S(2)}) async-start(), calls=%async_computation.19 | async-start | bytes 12582912 | tf_op jit(solution)/shard_map/psum | solution.py:299
  948.8 4.9 copy-start.9
  953.8 4.0 copy-start.14
  953.8 4.5 copy-start.22
  960.4 13.5 %copy-start.34 = (f32[256]{0:T(256)S(1)}, f32[256]{0:T(256)}, u32[]{:S(2)}) copy-start(f32[256]{0:T(256)} %param.22) | copy-start | bytes 3076
  960.4 37.7 %copy-start.26 = (f32[512,256]{1,0:T(8,128)S(1)}, f32[512,256]{1,0:T(8,128)}, u32[]{:S(2)}) copy-start(f32[512,256]{1,0:T(8,128)} %get-tuple-element.159) | copy-start | bytes 1572868
  1091.4 8.3 copy-start.23
  1094.5 6.4 copy-start.1
  (16 other events, 33.0 us)
Sparse Core Ops, SparseCore 0:
  35.6 108.9 reduce-scatter.9
  147.8 46.7 all-gather.1
  231.0 20.7 reduce-scatter.11
  254.2 144.2 reduce-scatter.17
  400.8 145.0 reduce-scatter.13
  694.5 19.2 reduce-scatter.19
  716.6 20.2 reduce-scatter.15
  750.0 43.8 reduce-scatter.21
  804.0 76.0 reduce-scatter.23
  948.9 18.4 reduce-scatter.25
  971.1 120.2 all-reduce.8
